TPU v7x, 32 devices: a whole 2x2x4 slice. The times are simulated.
32 devices in a mesh: col: 4 (over x, core), slab: 8 (over z, y).
Axes of the slice: x: 2, y: 2, z: 4, core: 2. Of those that a mesh axis runs over, the one named last changes fastest.
Arguments:
- labels: int32 [32, 64, 128], P('col', 'slab'), may hold values from 0 to 2
- table: float32 [3], replicated, may hold values from 0.3 to 3
- factor: float32 [32, 64, 128], P('col', 'slab'), may hold values from 0.5 to 2
- chi: float32 [3, 32, 64, 128], P(None, 'col', 'slab'), may hold values from -2.5 to 2.5
- weights: float32 [3, 3], replicated, may hold values from -3.5 to 3.5
Outputs:
- adjoint: float32 [3, 32, 64, 128], P(None, 'col', 'slab')
- gradient: float32 [32, 64, 128], P('col', 'slab')
All inputs are finite; a program needn't handle non-finite values.
Results may differ from a plain program's by a relative error of at most 0.0001.
Values sent between devices are 32-bit elements; how exact they have to be, the bound alone decides.
No kernel may reach another device: no remote copies, remote signals or barrier semaphores. Data moves between devices by JAX's collectives and lax.ppermute only.
A program may use at most 64 MiB of HBM per device.

v0:
```python
import jax
import jax.numpy as jnp
from jax import lax
from jax.sharding import PartitionSpec as P

ITERS = 3
mass_shift = 0.01


def extended(block, sides, width):
    for axis, dim in sides:
        count = lax.axis_size(axis)
        forward = [(i, i + 1) for i in range(count - 1)]
        forward.append((count - 1, 0))
        backward = [(target, source) for source, target in forward]
        low = lax.ppermute(
            lax.slice_in_dim(block, block.shape[dim] - width, None, axis=dim), axis, forward
        )
        high = lax.ppermute(lax.slice_in_dim(block, 0, width, axis=dim), axis, backward)
        block = jnp.concatenate([low, block, high], axis=dim)
    return block


def neighbour_pair(padded, field, spatial):
    if spatial == 0:
        return (padded[..., :-1, 1:-1, :], padded[..., 1:, 1:-1, :])
    if spatial == 1:
        return (padded[..., 1:-1, :-1, :], padded[..., 1:-1, 1:, :])
    return (field, jnp.roll(field, -1, axis=-1))


def split_faces(full, spatial):
    if spatial == 0:
        return (full[..., 1:, :, :], full[..., :-1, :, :])
    if spatial == 1:
        return (full[..., :, 1:, :], full[..., :, :-1, :])
    return (full, jnp.roll(full, 1, axis=-1))


def neighbours(padded, centre, spatial):
    if spatial == 0:
        return (padded[:, :-2, 1:-1, :], padded[:, 2:, 1:-1, :])
    if spatial == 1:
        return (padded[:, 1:-1, :-2, :], padded[:, 1:-1, 2:, :])
    return (jnp.roll(centre, 1, axis=-1), jnp.roll(centre, -1, axis=-1))


def widen(values):
    return values[:, None, None, None]


def apply_operator(padded, centre, cond_full):
    result = mass_shift * centre
    for d in range(3):
        c_now, c_prev = split_faces(cond_full[d], d)
        before, after = neighbours(padded, centre, d)
        result = result + c_now * (centre - after) + c_prev * (centre - before)
    return result


def squares(residual):
    return lax.psum(jnp.sum(residual * residual, axis=(1, 2, 3)), ("col", "slab"))


def shards(labels, table, factor, chi, weights):
    conduct = jnp.where(labels == 0, table[0], jnp.where(labels == 1, table[1], table[2])) * factor
    stacked = jnp.concatenate([chi, conduct[None]], axis=0)
    padded = extended(stacked, (("col", 1), ("slab", 2)), 1)
    chi_pad = padded[:3]
    cond_pad = padded[3]
    cond_full, strain_full, kpairs = ([], [], [])
    for d in range(3):
        here, after = neighbour_pair(cond_pad, conduct, d)
        cond_full.append(2.0 * here * after / (here + after))
        kpairs.append((here, after))
        c_here, c_after = neighbour_pair(chi_pad, chi, d)
        strain_full.append(
            jnp.stack([(1.0 if j == d else 0.0) + (c_after[j] - c_here[j]) for j in range(3)])
        )
    drive = jnp.zeros_like(chi)
    for d in range(3):
        flux_now, flux_prev = split_faces(cond_full[d] * strain_full[d], d)
        drive = drive + (flux_prev - flux_now)
    source = jnp.stack(
        [
            weights[i, 0] * drive[0] + weights[i, 1] * drive[1] + weights[i, 2] * drive[2]
            for i in range(3)
        ]
    )
    adjoint = jnp.zeros_like(source)
    residual = source
    direction = source
    norm_now = squares(residual)
    for step in range(ITERS):
        dir_pad = extended(direction, (("col", 1), ("slab", 2)), 1)
        image = apply_operator(dir_pad, direction, cond_full)
        curve = lax.psum(jnp.sum(direction * image, axis=(1, 2, 3)), ("col", "slab"))
        alpha = norm_now / curve
        adjoint = adjoint + widen(alpha) * direction
        residual = residual - widen(alpha) * image
        norm_next = squares(residual)
        direction = residual + widen(norm_next / norm_now) * direction
        norm_now = norm_next
    lam_pad = extended(adjoint, (("col", 1), ("slab", 2)), 1)
    gradient = jnp.zeros_like(conduct)
    for d in range(3):
        lam_here, lam_after = neighbour_pair(lam_pad, adjoint, d)
        lam_diff = lam_after - lam_here
        local = strain_full[d]
        energy = jnp.zeros_like(local[0])
        for i in range(3):
            for j in range(3):
                energy = energy + weights[i, j] * local[i] * local[j]
        h_term = energy - (lam_diff[0] * local[0] + lam_diff[1] * local[1] + lam_diff[2] * local[2])
        here, after = kpairs[d]
        square_sum = (here + after) ** 2
        part_here = 2.0 * after * after / square_sum
        part_after = 2.0 * here * here / square_sum
        term_now, unused_prev = split_faces(h_term * part_here, d)
        unused_now, term_prev = split_faces(h_term * part_after, d)
        gradient = gradient + term_now + term_prev
    return (adjoint, gradient)


def solution(mesh):
    in_specs = (
        P("col", "slab", None),
        P(),
        P("col", "slab", None),
        P(None, "col", "slab", None),
        P(),
    )
    out_specs = (P(None, "col", "slab", None), P("col", "slab", None))
    return jax.shard_map(shards, mesh=mesh, in_specs=in_specs, out_specs=out_specs, check_vma=False)
```

profile of v0, /device:TPU:0, one launch (start us, length us, event | category | flops | bytes accessed | tf_op | source)
XLA Modules:
  0.0 283.4 jit_solution(14369096348308002320)
XLA Ops:
  0.6 1.4 fusion.147
  2.0 2.6 select_multiply_fusion
  4.6 0.5 collective-permute-start
  5.1 2.0 collective-permute-start.1
  7.1 0.1 slice.582
  7.2 0.1 slice.488
  7.3 0.1 fusion.92
  7.4 0.1 fusion.118
  7.5 0.7 copy-done.2
  8.2 0.7 fusion.146
  8.9 0.1 slice.601
  9.0 0.1 slice.588
  9.1 5.4 %collective-permute-start.3 = (f32[4,10,1,128]{3,2,1,0:T(1,128)S(1)}, f32[4,10,1,128]{3,2,1,0:T(1,128)S(1)}, u32[]{:S(2)}, u32[]{:S(2)}) collective-permute-start(f32[4,10,1,128]{3,2,1,0:T(1,128)S(1)} %get-tuple-element.19), channel_id=1, source_target_pairs={{1,0},{2,1},{3,2},{4,3},{5,4},{6,5},{7,6},{0,7},{9,8},{10,9},{11,1... | collective-permute-start | bytes 61448 | tf_op jit(solution)/shard_map/ppermute | solution.py:19
  14.5 1.5 collective-permute-done.3
  15.9 5.1 %collective-permute-done.2 = f32[4,10,1,128]{3,2,1,0:T(1,128)S(1)} collective-permute-done((f32[4,10,1,128]{3,2,1,0:T(1,128)S(1)}, f32[4,10,1,128]{3,2,1,0:T(1,128)S(1)}, u32[]{:S(2)}, u32[]{:S(2)}) %collective-permute-start.2) | collective-permute-done | bytes 20512 | tf_op jit(solution)/shard_map/ppermute | solution.py:16
  21.2 0.1 fusion.46
  21.3 5.6 %multiply_add_fusion.5 = (f32[1,8,8,128]{3,2,1,0:T(8,128)S(1)}, f32[1,8,8,128]{3,2,1,0:T(8,128)S(1)}, f32[1,8,8,128]{3,2,1,0:T(8,128)S(1)}) fusion(f32[3,8,8,128]{3,2,1,0:T(8,128)S(1)} %fusion.46, f32[]{:T(128)} %bitcast.7, f32[]{:T(128)} %bitcast.6, f32[]{:T(128)} %bitcast, f32[]{:T(128)} %bitcast.10, f32[]{:T(128)} %bitcast.9, f32[]{:T(128)} %bitcast.8, ...), kind=kLoop, calls=%fused_computation.280 | loop fusion | flops 122880 | bytes 196644 | tf_op jit(solution)/shard_map/add | solution.py:86
  27.0 0.1 fusion.141
  27.1 0.1 fusion.140
  27.3 1.7 collective-permute-start.4
  29.0 0.1 fusion.144
  29.1 1.3 collective-permute-done.5
  30.4 0.1 collective-permute-start.6
  30.5 2.0 collective-permute-start.7
  32.5 1.7 collective-permute-done.6
  34.2 2.8 collective-permute-done.7
  37.0 0.3 multiply_reduce_fusion.3
  37.2 36.9 %all-reduce = (f32[3]{0:T(128)S(1)}, f32[3]{0:T(128)S(1)}) all-reduce(f32[3]{0:T(128)S(1)} %get-tuple-element.3, f32[3]{0:T(128)S(1)} %get-tuple-element.2), channel_id=1, replica_groups=mesh['col'=4,'slab'=8] {'col','slab'}, use_global_device_ids=true, to_apply=%region_1.2 | all-reduce | flops 6 | bytes 48 | tf_op jit(solution)/shard_map/psum | solution.py:62
  74.1 0.2 multiply_reduce_fusion.2
  74.3 42.2 %psum.44 = f32[3]{0:T(128)S(1)} all-reduce(f32[3]{0:T(128)S(1)} %get-tuple-element.10), channel_id=1, replica_groups=mesh['col'=4,'slab'=8] {'col','slab'}, use_global_device_ids=true, to_apply=%region_5.6 | all-reduce | flops 3 | bytes 24 | tf_op jit(solution)/shard_map/psum | solution.py:62
  116.5 0.1 multiply_add_fusion.2
  116.7 1.7 collective-permute-start.8
  118.4 0.1 fusion.137
  118.5 1.3 collective-permute-done.9
  119.9 3.3 %collective-permute-start.10 = (f32[3,10,1,128]{3,2,1,0:T(1,128)S(1)}, f32[3,10,1,128]{3,2,1,0:T(1,128)S(1)}, u32[]{:S(2)}, u32[]{:S(2)}) collective-permute-start(f32[3,10,1,128]{3,2,1,0:T(1,128)S(1)} %get-tuple-element.27), channel_id=1, source_target_pairs={{1,0},{2,1},{3,2},{4,3},{5,4},{6,5},{7,6},{0,7},{9,8},{10,9},{11,1... | collective-permute-start | bytes 46088 | tf_op jit(solution)/shard_map/ppermute | solution.py:19
  123.2 0.1 fusion.138
  123.3 1.3 collective-permute-done.10
  124.6 5.0 %collective-permute-done.11 = f32[3,10,1,128]{3,2,1,0:T(1,128)S(1)} collective-permute-done((f32[3,10,1,128]{3,2,1,0:T(1,128)S(1)}, f32[3,10,1,128]{3,2,1,0:T(1,128)S(1)}, u32[]{:S(2)}, u32[]{:S(2)}) %collective-permute-start.11) | collective-permute-done | bytes 15392 | tf_op jit(solution)/shard_map/ppermute | solution.py:16
  129.6 0.2 multiply_reduce_fusion.1
  129.8 36.8 %psum.45 = f32[3]{0:T(128)S(1)} all-reduce(f32[3]{0:T(128)S(1)} %get-tuple-element.8), channel_id=1, replica_groups=mesh['col'=4,'slab'=8] {'col','slab'}, use_global_device_ids=true, to_apply=%region_7.8 | all-reduce | flops 3 | bytes 24 | tf_op jit(solution)/shard_map/psum | solution.py:97
  166.7 0.2 multiply_reduce_fusion
  166.9 41.4 %psum.46 = f32[3]{0:T(128)S(1)} all-reduce(f32[3]{0:T(128)S(1)} %multiply_reduce_fusion), channel_id=1, replica_groups=mesh['col'=4,'slab'=8] {'col','slab'}, use_global_device_ids=true, to_apply=%region_9.10 | all-reduce | flops 3 | bytes 24 | tf_op jit(solution)/shard_map/psum | solution.py:62
  208.3 0.1 multiply_add_fusion.1
  208.5 1.7 collective-permute-start.12
  210.2 0.1 fusion.133
  210.3 1.3 collective-permute-done.13
  211.7 3.3 %collective-permute-start.14 = (f32[3,10,1,128]{3,2,1,0:T(1,128)S(1)}, f32[3,10,1,128]{3,2,1,0:T(1,128)S(1)}, u32[]{:S(2)}, u32[]{:S(2)}) collective-permute-start(f32[3,10,1,128]{3,2,1,0:T(1,128)S(1)} %get-tuple-element.25), channel_id=1, source_target_pairs={{1,0},{2,1},{3,2},{4,3},{5,4},{6,5},{7,6},{0,7},{9,8},{10,9},{11,1... | collective-permute-start | bytes 46088 | tf_op jit(solution)/shard_map/ppermute | solution.py:19
  215.0 0.1 fusion.134
  215.1 1.3 collective-permute-done.14
  216.4 5.0 %collective-permute-done.15 = f32[3,10,1,128]{3,2,1,0:T(1,128)S(1)} collective-permute-done((f32[3,10,1,128]{3,2,1,0:T(1,128)S(1)}, f32[3,10,1,128]{3,2,1,0:T(1,128)S(1)}, u32[]{:S(2)}, u32[]{:S(2)}) %collective-permute-start.15) | collective-permute-done | bytes 15392 | tf_op jit(solution)/shard_map/ppermute | solution.py:16
  221.4 0.2 fusion.7
  221.6 36.8 %psum.47 = f32[3]{0:T(128)S(1)} all-reduce(f32[3]{0:T(128)S(1)} %fusion.7), channel_id=1, replica_groups=mesh['col'=4,'slab'=8] {'col','slab'}, use_global_device_ids=true, to_apply=%region_11.12 | all-reduce | flops 3 | bytes 24 | tf_op jit(solution)/shard_map/psum | solution.py:97
  258.5 0.1 multiply_add_fusion
  258.6 0.1 slice.639
  258.7 0.1 collective-permute-start.17
  258.8 1.7 collective-permute-start.16
  260.5 0.1 maximum_subtract_fusion.8
  260.6 5.7 %fusion.94 = (f32[8,8,128]{2,1,0:T(8,128)S(1)}, f32[8,8,128]{2,1,0:T(8,128)S(1)}) fusion(f32[8,8,128]{2,1,0:T(8,128)S(1)} %select_multiply_fusion, f32[8,8,1]{2,1,0:T(8,128)S(1)} %bitcast.219, f32[8,8,127]{2,1,0:T(8,128)S(1)} %slice.582, f32[3,8,8,128]{3,2,1,0:T(8,128)S(1)} %maximum_subtract_fusion.8, f32[]{:T(128)} %bitcast.13, f32[]{:T(128)} %bitcast.12, ...), kind=kLoop, calls=%fused_computation.222 | loop fusion | flops 319488 | bytes 327716 | tf_op jit(solution)/shard_map/mul | solution.py:120
  266.3 0.1 slice.644
  266.4 4.0 %collective-permute-start.18 = (f32[3,10,1,128]{3,2,1,0:T(1,128)S(1)}, f32[3,10,1,128]{3,2,1,0:T(1,128)S(1)}, u32[]{:S(2)}, u32[]{:S(2)}) collective-permute-start(f32[3,10,1,128]{3,2,1,0:T(1,128)S(1)} %get-tuple-element.23), channel_id=1, source_target_pairs={{1,0},{2,1},{3,2},{4,3},{5,4},{6,5},{7,6},{0,7},{9,8},{10,9},{11,1... | collective-permute-start | bytes 46088 | tf_op jit(solution)/shard_map/ppermute | solution.py:19
  270.5 5.7 %fusion.81 = f32[9,8,128]{2,1,0:T(8,128)S(1)} fusion(f32[3,9,8,128]{3,2,1,0:T(8,128)S(1)} %maximum_subtract_fusion, f32[1,9,8,128]{3,2,1,0:T(8,128)S(1)} %get-tuple-element.18, f32[1,9,8,128]{3,2,1,0:T(8,128)S(1)} %get-tuple-element.17, f32[1,9,8,128]{3,2,1,0:T(8,128)S(1)} %get-tuple-element.16, f32[]{:T(128)} %bitcast.13, f32[]{:T(128)} %bitcast.12, ...), kind=kLoop, calls=%fused_computation.190 | loop fusion | flops 294912 | bytes 258084 | tf_op jit(solution)/shard_map/sub | solution.py:114
  276.2 0.7 collective-permute-done.19
  276.9 5.7 %fusion.62 = f32[8,9,128]{2,1,0:T(8,128)S(1)} fusion(f32[3,8,9,128]{3,2,1,0:T(8,128)S(1)} %fusion, f32[1,8,9,128]{3,2,1,0:T(8,128)S(1)} %fusion.68, f32[1,8,9,128]{3,2,1,0:T(8,128)S(1)} %fusion.69, f32[1,8,9,128]{3,2,1,0:T(8,128)S(1)} %maximum_subtract_fusion.10, f32[]{:T(128)} %bitcast.13, f32[]{:T(128)} %bitcast.12, f32[]{:T(128)} %bitcast.11, ...), kind=kLoop, calls=%fused_computation.137 | loop fusion | flops 294912 | bytes 258084 | tf_op jit(solution)/shard_map/sub | solution.py:114
  282.6 0.7 fusion.101
  (49 shorter events, 0.7 us)
Async XLA Ops:
  0.6 4.0 %copy-start = (f32[3,8,8,128]{3,2,1,0:T(8,128)S(1)}, f32[3,8,8,128]{3,2,1,0:T(8,128)}, u32[]{:S(2)}) copy-start(f32[3,8,8,128]{3,2,1,0:T(8,128)} %param.8) | copy-start | bytes 294916
  4.6 4.4 %collective-permute-start = (f32[4,1,8,128]{3,2,1,0:T(8,128)S(1)}, f32[4,1,8,128]{3,2,1,0:T(8,128)S(1)}, u32[]{:S(2)}, u32[]{:S(2)}) collective-permute-start(f32[4,1,8,128]{3,2,1,0:T(8,128)S(1)} %get-tuple-element.21), channel_id=1, source_target_pairs={{0,8},{8,16},{16,24},{24,0},{1,9},{9,17},{17,25},{25,1},{2,10},{10... | collective-permute-start | bytes 49160 | tf_op jit(solution)/shard_map/ppermute | solution.py:16
  5.1 3.9 %collective-permute-start.1 = (f32[4,1,8,128]{3,2,1,0:T(8,128)S(1)}, f32[4,1,8,128]{3,2,1,0:T(8,128)S(1)}, u32[]{:S(2)}, u32[]{:S(2)}) collective-permute-start(f32[4,1,8,128]{3,2,1,0:T(8,128)S(1)} %get-tuple-element.22), channel_id=1, source_target_pairs={{8,0},{16,8},{24,16},{0,24},{9,1},{17,9},{25,17},{1,25},{10,2},{18... | collective-permute-start | bytes 49160 | tf_op jit(solution)/shard_map/ppermute | solution.py:19
  7.5 0.7 copy-start.2
  9.1 6.8 %collective-permute-start.3 = (f32[4,10,1,128]{3,2,1,0:T(1,128)S(1)}, f32[4,10,1,128]{3,2,1,0:T(1,128)S(1)}, u32[]{:S(2)}, u32[]{:S(2)}) collective-permute-start(f32[4,10,1,128]{3,2,1,0:T(1,128)S(1)} %get-tuple-element.19), channel_id=1, source_target_pairs={{1,0},{2,1},{3,2},{4,3},{5,4},{6,5},{7,6},{0,7},{9,8},{10,9},{11,1... | collective-permute-start | bytes 61448 | tf_op jit(solution)/shard_map/ppermute | solution.py:19
  14.5 6.5 %collective-permute-start.2 = (f32[4,10,1,128]{3,2,1,0:T(1,128)S(1)}, f32[4,10,1,128]{3,2,1,0:T(1,128)S(1)}, u32[]{:S(2)}, u32[]{:S(2)}) collective-permute-start(f32[4,10,1,128]{3,2,1,0:T(1,128)S(1)} %get-tuple-element.20), channel_id=1, source_target_pairs={{0,1},{1,2},{2,3},{3,4},{4,5},{5,6},{6,7},{7,0},{8,9},{9,10},{10,1... | collective-permute-start | bytes 61448 | tf_op jit(solution)/shard_map/ppermute | solution.py:16
  27.2 3.2 %collective-permute-start.5 = (f32[3,1,8,128]{3,2,1,0:T(8,128)S(1)}, f32[3,1,8,128]{3,2,1,0:T(8,128)S(1)}, u32[]{:S(2)}, u32[]{:S(2)}) collective-permute-start(f32[3,1,8,128]{3,2,1,0:T(8,128)S(1)} %get-tuple-element.45), channel_id=1, source_target_pairs={{0,8},{8,16},{16,24},{24,0},{1,9},{9,17},{17,25},{25,1},{2,10},{10... | collective-permute-start | bytes 36872 | tf_op jit(solution)/shard_map/ppermute | solution.py:16
  27.3 3.1 %collective-permute-start.4 = (f32[3,1,8,128]{3,2,1,0:T(8,128)S(1)}, f32[3,1,8,128]{3,2,1,0:T(8,128)S(1)}, u32[]{:S(2)}, u32[]{:S(2)}) collective-permute-start(f32[3,1,8,128]{3,2,1,0:T(8,128)S(1)} %get-tuple-element.46), channel_id=1, source_target_pairs={{8,0},{16,8},{24,16},{0,24},{9,1},{17,9},{25,17},{1,25},{10,2},{18... | collective-permute-start | bytes 36872 | tf_op jit(solution)/shard_map/ppermute | solution.py:19
  30.4 3.8 %collective-permute-start.6 = (f32[3,10,1,128]{3,2,1,0:T(1,128)S(1)}, f32[3,10,1,128]{3,2,1,0:T(1,128)S(1)}, u32[]{:S(2)}, u32[]{:S(2)}) collective-permute-start(f32[3,10,1,128]{3,2,1,0:T(1,128)S(1)} %get-tuple-element.29), channel_id=1, source_target_pairs={{1,0},{2,1},{3,2},{4,3},{5,4},{6,5},{7,6},{0,7},{9,8},{10,9},{11,1... | collective-permute-start | bytes 46088 | tf_op jit(solution)/shard_map/ppermute | solution.py:19
  30.5 6.5 %collective-permute-start.7 = (f32[3,10,1,128]{3,2,1,0:T(1,128)S(1)}, f32[3,10,1,128]{3,2,1,0:T(1,128)S(1)}, u32[]{:S(2)}, u32[]{:S(2)}) collective-permute-start(f32[3,10,1,128]{3,2,1,0:T(1,128)S(1)} %get-tuple-element.30), channel_id=1, source_target_pairs={{0,1},{1,2},{2,3},{3,4},{4,5},{5,6},{6,7},{7,0},{8,9},{9,10},{10,1... | collective-permute-start | bytes 46088 | tf_op jit(solution)/shard_map/ppermute | solution.py:16
  116.6 3.2 %collective-permute-start.9 = (f32[3,1,8,128]{3,2,1,0:T(8,128)S(1)}, f32[3,1,8,128]{3,2,1,0:T(8,128)S(1)}, u32[]{:S(2)}, u32[]{:S(2)}) collective-permute-start(f32[3,1,8,128]{3,2,1,0:T(8,128)S(1)} %get-tuple-element.39), channel_id=1, source_target_pairs={{0,8},{8,16},{16,24},{24,0},{1,9},{9,17},{17,25},{25,1},{2,10},{10... | collective-permute-start | bytes 36872 | tf_op jit(solution)/shard_map/ppermute | solution.py:16
  116.7 3.1 %collective-permute-start.8 = (f32[3,1,8,128]{3,2,1,0:T(8,128)S(1)}, f32[3,1,8,128]{3,2,1,0:T(8,128)S(1)}, u32[]{:S(2)}, u32[]{:S(2)}) collective-permute-start(f32[3,1,8,128]{3,2,1,0:T(8,128)S(1)} %get-tuple-element.40), channel_id=1, source_target_pairs={{8,0},{16,8},{24,16},{0,24},{9,1},{17,9},{25,17},{1,25},{10,2},{18... | collective-permute-start | bytes 36872 | tf_op jit(solution)/shard_map/ppermute | solution.py:19
  119.9 4.7 %collective-permute-start.10 = (f32[3,10,1,128]{3,2,1,0:T(1,128)S(1)}, f32[3,10,1,128]{3,2,1,0:T(1,128)S(1)}, u32[]{:S(2)}, u32[]{:S(2)}) collective-permute-start(f32[3,10,1,128]{3,2,1,0:T(1,128)S(1)} %get-tuple-element.27), channel_id=1, source_target_pairs={{1,0},{2,1},{3,2},{4,3},{5,4},{6,5},{7,6},{0,7},{9,8},{10,9},{11,1... | collective-permute-start | bytes 46088 | tf_op jit(solution)/shard_map/ppermute | solution.py:19
  123.2 6.4 %collective-permute-start.11 = (f32[3,10,1,128]{3,2,1,0:T(1,128)S(1)}, f32[3,10,1,128]{3,2,1,0:T(1,128)S(1)}, u32[]{:S(2)}, u32[]{:S(2)}) collective-permute-start(f32[3,10,1,128]{3,2,1,0:T(1,128)S(1)} %get-tuple-element.28), channel_id=1, source_target_pairs={{0,1},{1,2},{2,3},{3,4},{4,5},{5,6},{6,7},{7,0},{8,9},{9,10},{10,1... | collective-permute-start | bytes 46088 | tf_op jit(solution)/shard_map/ppermute | solution.py:16
  208.4 3.2 %collective-permute-start.13 = (f32[3,1,8,128]{3,2,1,0:T(8,128)S(1)}, f32[3,1,8,128]{3,2,1,0:T(8,128)S(1)}, u32[]{:S(2)}, u32[]{:S(2)}) collective-permute-start(f32[3,1,8,128]{3,2,1,0:T(8,128)S(1)} %get-tuple-element.37), channel_id=1, source_target_pairs={{0,8},{8,16},{16,24},{24,0},{1,9},{9,17},{17,25},{25,1},{2,10},{10... | collective-permute-start | bytes 36872 | tf_op jit(solution)/shard_map/ppermute | solution.py:16
  208.5 3.1 %collective-permute-start.12 = (f32[3,1,8,128]{3,2,1,0:T(8,128)S(1)}, f32[3,1,8,128]{3,2,1,0:T(8,128)S(1)}, u32[]{:S(2)}, u32[]{:S(2)}) collective-permute-start(f32[3,1,8,128]{3,2,1,0:T(8,128)S(1)} %get-tuple-element.38), channel_id=1, source_target_pairs={{8,0},{16,8},{24,16},{0,24},{9,1},{17,9},{25,17},{1,25},{10,2},{18... | collective-permute-start | bytes 36872 | tf_op jit(solution)/shard_map/ppermute | solution.py:19
  211.7 4.7 %collective-permute-start.14 = (f32[3,10,1,128]{3,2,1,0:T(1,128)S(1)}, f32[3,10,1,128]{3,2,1,0:T(1,128)S(1)}, u32[]{:S(2)}, u32[]{:S(2)}) collective-permute-start(f32[3,10,1,128]{3,2,1,0:T(1,128)S(1)} %get-tuple-element.25), channel_id=1, source_target_pairs={{1,0},{2,1},{3,2},{4,3},{5,4},{6,5},{7,6},{0,7},{9,8},{10,9},{11,1... | collective-permute-start | bytes 46088 | tf_op jit(solution)/shard_map/ppermute | solution.py:19
  215.0 6.4 %collective-permute-start.15 = (f32[3,10,1,128]{3,2,1,0:T(1,128)S(1)}, f32[3,10,1,128]{3,2,1,0:T(1,128)S(1)}, u32[]{:S(2)}, u32[]{:S(2)}) collective-permute-start(f32[3,10,1,128]{3,2,1,0:T(1,128)S(1)} %get-tuple-element.26), channel_id=1, source_target_pairs={{0,1},{1,2},{2,3},{3,4},{4,5},{5,6},{6,7},{7,0},{8,9},{9,10},{10,1... | collective-permute-start | bytes 46088 | tf_op jit(solution)/shard_map/ppermute | solution.py:16
  258.6 18.3 %copy-start.1 = (f32[3,8,8,128]{3,2,1,0:T(8,128)}, f32[3,8,8,128]{3,2,1,0:T(8,128)S(1)}, u32[]{:S(2)}) copy-start(f32[3,8,8,128]{3,2,1,0:T(8,128)S(1)} %multiply_add_fusion) | copy-start | bytes 294916
  258.7 7.7 %collective-permute-start.17 = (f32[3,1,8,128]{3,2,1,0:T(8,128)S(1)}, f32[3,1,8,128]{3,2,1,0:T(8,128)S(1)}, u32[]{:S(2)}, u32[]{:S(2)}) collective-permute-start(f32[3,1,8,128]{3,2,1,0:T(8,128)S(1)} %get-tuple-element.31), channel_id=1, source_target_pairs={{0,8},{8,16},{16,24},{24,0},{1,9},{9,17},{17,25},{25,1},{2,10},{10... | collective-permute-start | bytes 36872 | tf_op jit(solution)/shard_map/ppermute | solution.py:16
  258.8 7.6 %collective-permute-start.16 = (f32[3,1,8,128]{3,2,1,0:T(8,128)S(1)}, f32[3,1,8,128]{3,2,1,0:T(8,128)S(1)}, u32[]{:S(2)}, u32[]{:S(2)}) collective-permute-start(f32[3,1,8,128]{3,2,1,0:T(8,128)S(1)} %get-tuple-element.32), channel_id=1, source_target_pairs={{8,0},{16,8},{24,16},{0,24},{9,1},{17,9},{25,17},{1,25},{10,2},{18... | collective-permute-start | bytes 36872 | tf_op jit(solution)/shard_map/ppermute | solution.py:19
  266.4 9.7 %collective-permute-start.18 = (f32[3,10,1,128]{3,2,1,0:T(1,128)S(1)}, f32[3,10,1,128]{3,2,1,0:T(1,128)S(1)}, u32[]{:S(2)}, u32[]{:S(2)}) collective-permute-start(f32[3,10,1,128]{3,2,1,0:T(1,128)S(1)} %get-tuple-element.23), channel_id=1, source_target_pairs={{1,0},{2,1},{3,2},{4,3},{5,4},{6,5},{7,6},{0,7},{9,8},{10,9},{11,1... | collective-permute-start | bytes 46088 | tf_op jit(solution)/shard_map/ppermute | solution.py:19
  270.5 6.4 %collective-permute-start.19 = (f32[3,10,1,128]{3,2,1,0:T(1,128)S(1)}, f32[3,10,1,128]{3,2,1,0:T(1,128)S(1)}, u32[]{:S(2)}, u32[]{:S(2)}) collective-permute-start(f32[3,10,1,128]{3,2,1,0:T(1,128)S(1)} %get-tuple-element.24), channel_id=1, source_target_pairs={{0,1},{1,2},{2,3},{3,4},{4,5},{5,6},{6,7},{7,0},{8,9},{9,10},{10,1... | collective-permute-start | bytes 46088 | tf_op jit(solution)/shard_map/ppermute | solution.py:16
where the time goes:
time: 285 us; the launch traced here: 283 us
  blocking collectives  194 us (68%)
  other arithmetic  28.3 us (10%)
  waiting for transfers between devices  28.3 us (10%)
  starting transfers between devices  27.8 us (10%)
  local copies, waits for them, and re-layouts  3.7 us (1%)
    psum x3, blocking collectives, squares(): lax.psum(jnp.sum(residual * residual, axis=(1, 2, 3)), ('col', 'slab'))  121 us
    psum x2, blocking collectives, shards(): lax.psum(jnp.sum(direction * image, axis=(1, 2, 3)), ('col', 'slab'))  73.7 us
    ppermute x10, starting transfers between devices, extended(): lax.ppermute(lax.slice_in_dim(block, 0, width, axis=dim), axis, backward)  25 us
    ppermute x10, waiting for transfers between devices, extended(): lax.ppermute(lax.slice_in_dim(block, block.shape[dim] - width, None, axis...  22.4 us
    sub x2, other arithmetic, shards(): energy - (lam_diff[0] * local[0] + lam_diff[1] * local[1] + lam_diff[2] *...  11.4 us
    ppermute x10, waiting for transfers between devices, extended(): lax.ppermute(lax.slice_in_dim(block, 0, width, axis=dim), axis, backward)  5.95 us
    mul x1, other arithmetic, shards(): unused_now, term_prev = split_faces(h_term * part_after, d)  5.72 us
  transfers between devices with their start and end apart: 20, of which 12 were waited for; matrix products, arithmetic and copies ran while one was open for 5% of the time, Pallas kernels for 0%

commit v1 on v0

--- a/solution.py
+++ b/solution.py
@@ -94,7 +94,9 @@
     for step in range(ITERS):
         dir_pad = extended(direction, (("col", 1), ("slab", 2)), 1)
         image = apply_operator(dir_pad, direction, cond_full)
-        curve = lax.psum(jnp.sum(direction * image, axis=(1, 2, 3)), ("col", "slab"))
+        curve = jnp.sum(direction * image, axis=(1, 2, 3))
+        for mesh_axis in ("slab", "col"):
+            curve = lax.psum(curve, mesh_axis)
         alpha = norm_now / curve
         adjoint = adjoint + widen(alpha) * direction
         residual = residual - widen(alpha) * image

time: 285 us -> 276 us (0.968)
  blocking collectives: 194 us -> 187 us
    psum x2 -> x6, blocking collectives: 73.7 us -> 68.4 us  [shards(): curve = lax.psum(curve, mesh_axis)]
where the time goes in v1:
time: 276 us; the launch traced here: 275 us
  blocking collectives  187 us (68%)
  waiting for transfers between devices  28.3 us (10%)
  other arithmetic  28.1 us (10%)
  starting transfers between devices  26.6 us (10%)
  local copies, waits for them, and re-layouts  3.69 us (1%)
    psum x3, blocking collectives, squares(): lax.psum(jnp.sum(residual * residual, axis=(1, 2, 3)), ('col', 'slab'))  118 us
    psum x6, blocking collectives, shards(): curve = lax.psum(curve, mesh_axis)  68.4 us
    ppermute x10, starting transfers between devices, extended(): lax.ppermute(lax.slice_in_dim(block, 0, width, axis=dim), axis, backward)  23.8 us
    ppermute x10, waiting for transfers between devices, extended(): lax.ppermute(lax.slice_in_dim(block, block.shape[dim] - width, None, axis...  22.4 us
    sub x2, other arithmetic, shards(): energy - (lam_diff[0] * local[0] + lam_diff[1] * local[1] + lam_diff[2] *...  11.3 us
    ppermute x10, waiting for transfers between devices, extended(): lax.ppermute(lax.slice_in_dim(block, 0, width, axis=dim), axis, backward)  5.95 us
    mul x1, other arithmetic, shards(): unused_now, term_prev = split_faces(h_term * part_after, d)  5.67 us
    add x1, other arithmetic, shards(): weights[i, 0] * drive[0] + weights[i, 1] * drive[1]  5.6 us
  transfers between devices with their start and end apart: 20, of which 12 were waited for; matrix products, arithmetic and copies ran while one was open for 5% of the time, Pallas kernels for 0%

profile of v1, /device:TPU:0, one launch (start us, length us, event | category | flops | bytes accessed | tf_op | source)
XLA Modules:
  0.0 274.5 jit_solution(13815061697196058793)
XLA Ops:
  0.6 1.3 fusion.147
  2.0 2.6 select_multiply_fusion
  4.6 0.5 collective-permute-start
  5.1 2.0 collective-permute-start.1
  7.2 0.1 slice.488
  7.3 0.1 fusion.92
  7.4 0.1 fusion.118
  7.5 0.7 copy-done.2
  8.2 0.7 fusion.146
  8.9 0.1 slice.588
  9.1 5.4 %collective-permute-start.3 = (f32[4,10,1,128]{3,2,1,0:T(1,128)S(1)}, f32[4,10,1,128]{3,2,1,0:T(1,128)S(1)}, u32[]{:S(2)}, u32[]{:S(2)}) collective-permute-start(f32[4,10,1,128]{3,2,1,0:T(1,128)S(1)} %get-tuple-element.17), channel_id=1, source_target_pairs={{1,0},{2,1},{3,2},{4,3},{5,4},{6,5},{7,6},{0,7},{9,8},{10,9},{11,1... | collective-permute-start | bytes 61448 | tf_op jit(solution)/shard_map/ppermute | solution.py:19
  14.5 1.5 collective-permute-done.3
  15.9 5.1 %collective-permute-done.2 = f32[4,10,1,128]{3,2,1,0:T(1,128)S(1)} collective-permute-done((f32[4,10,1,128]{3,2,1,0:T(1,128)S(1)}, f32[4,10,1,128]{3,2,1,0:T(1,128)S(1)}, u32[]{:S(2)}, u32[]{:S(2)}) %collective-permute-start.2) | collective-permute-done | bytes 20512 | tf_op jit(solution)/shard_map/ppermute | solution.py:16
  21.2 0.1 fusion.46
  21.3 5.6 %multiply_add_fusion.5 = (f32[1,8,8,128]{3,2,1,0:T(8,128)S(1)}, f32[1,8,8,128]{3,2,1,0:T(8,128)S(1)}, f32[1,8,8,128]{3,2,1,0:T(8,128)S(1)}) fusion(f32[3,8,8,128]{3,2,1,0:T(8,128)S(1)} %fusion.46, f32[]{:T(128)} %bitcast.7, f32[]{:T(128)} %bitcast.6, f32[]{:T(128)} %bitcast, f32[]{:T(128)} %bitcast.10, f32[]{:T(128)} %bitcast.9, f32[]{:T(128)} %bitcast.8, ...), kind=kLoop, calls=%fused_computation.280 | loop fusion | flops 122880 | bytes 196644 | tf_op jit(solution)/shard_map/add | solution.py:86
  27.0 0.1 fusion.141
  27.1 0.1 fusion.140
  27.2 1.7 collective-permute-start.4
  28.9 0.1 fusion.144
  29.0 1.3 collective-permute-done.5
  30.4 2.0 collective-permute-start.7
  32.5 1.7 collective-permute-done.6
  34.2 2.8 %collective-permute-done.7 = f32[3,10,1,128]{3,2,1,0:T(1,128)S(1)} collective-permute-done((f32[3,10,1,128]{3,2,1,0:T(1,128)S(1)}, f32[3,10,1,128]{3,2,1,0:T(1,128)S(1)}, u32[]{:S(2)}, u32[]{:S(2)}) %collective-permute-start.7) | collective-permute-done | bytes 15392 | tf_op jit(solution)/shard_map/ppermute | solution.py:16
  36.9 0.3 multiply_reduce_fusion.3
  37.2 17.1 %psum.64 = f32[3]{0:T(128)S(1)} all-reduce(f32[3]{0:T(128)S(1)} %get-tuple-element.2), channel_id=1, replica_groups=mesh['col'=4,'slab'=8] {'slab'}, use_global_device_ids=true, to_apply=%region_3.4 | all-reduce | flops 3 | bytes 24 | tf_op jit(solution)/shard_map/psum | solution.py:99
  54.3 5.6 %psum.65 = f32[3]{0:T(128)S(1)} all-reduce(f32[3]{0:T(128)S(1)} %psum.64), channel_id=1, replica_groups=mesh['col'=4,'slab'=8] {'col'}, use_global_device_ids=true, to_apply=%region_4.5 | all-reduce | flops 3 | bytes 24 | tf_op jit(solution)/shard_map/psum | solution.py:99
  59.9 38.6 %psum.63 = f32[3]{0:T(128)S(1)} all-reduce(f32[3]{0:T(128)S(1)} %get-tuple-element.3), channel_id=1, replica_groups=mesh['col'=4,'slab'=8] {'col','slab'}, use_global_device_ids=true, to_apply=%region_1.2 | all-reduce | flops 3 | bytes 24 | tf_op jit(solution)/shard_map/psum | solution.py:62
  98.6 0.2 multiply_reduce_fusion.2
  98.8 41.1 %psum.66 = f32[3]{0:T(128)S(1)} all-reduce(f32[3]{0:T(128)S(1)} %get-tuple-element.8), channel_id=1, replica_groups=mesh['col'=4,'slab'=8] {'col','slab'}, use_global_device_ids=true, to_apply=%region_6.7 | all-reduce | flops 3 | bytes 24 | tf_op jit(solution)/shard_map/psum | solution.py:62
  139.8 0.1 multiply_add_fusion.2
  140.0 1.7 collective-permute-start.8
  141.7 0.1 fusion.137
  141.8 1.3 collective-permute-done.9
  143.2 3.3 %collective-permute-start.10 = (f32[3,10,1,128]{3,2,1,0:T(1,128)S(1)}, f32[3,10,1,128]{3,2,1,0:T(1,128)S(1)}, u32[]{:S(2)}, u32[]{:S(2)}) collective-permute-start(f32[3,10,1,128]{3,2,1,0:T(1,128)S(1)} %get-tuple-element.25), channel_id=1, source_target_pairs={{1,0},{2,1},{3,2},{4,3},{5,4},{6,5},{7,6},{0,7},{9,8},{10,9},{11,1... | collective-permute-start | bytes 46088 | tf_op jit(solution)/shard_map/ppermute | solution.py:19
  146.5 0.1 fusion.138
  146.6 1.3 collective-permute-done.10
  147.9 5.0 %collective-permute-done.11 = f32[3,10,1,128]{3,2,1,0:T(1,128)S(1)} collective-permute-done((f32[3,10,1,128]{3,2,1,0:T(1,128)S(1)}, f32[3,10,1,128]{3,2,1,0:T(1,128)S(1)}, u32[]{:S(2)}, u32[]{:S(2)}) %collective-permute-start.11) | collective-permute-done | bytes 15392 | tf_op jit(solution)/shard_map/ppermute | solution.py:16
  152.9 0.2 multiply_reduce_fusion.1
  153.1 17.1 %psum.67 = f32[3]{0:T(128)S(1)} all-reduce(f32[3]{0:T(128)S(1)} %get-tuple-element.6), channel_id=1, replica_groups=mesh['col'=4,'slab'=8] {'slab'}, use_global_device_ids=true, to_apply=%region_8.9 | all-reduce | flops 3 | bytes 24 | tf_op jit(solution)/shard_map/psum | solution.py:99
  170.3 5.6 %psum.68 = f32[3]{0:T(128)S(1)} all-reduce(f32[3]{0:T(128)S(1)} %psum.67), channel_id=1, replica_groups=mesh['col'=4,'slab'=8] {'col'}, use_global_device_ids=true, to_apply=%region_9.10 | all-reduce | flops 3 | bytes 24 | tf_op jit(solution)/shard_map/psum | solution.py:99
  175.9 0.2 multiply_reduce_fusion
  176.1 38.7 %psum.69 = f32[3]{0:T(128)S(1)} all-reduce(f32[3]{0:T(128)S(1)} %multiply_reduce_fusion), channel_id=1, replica_groups=mesh['col'=4,'slab'=8] {'col','slab'}, use_global_device_ids=true, to_apply=%region_11.12 | all-reduce | flops 3 | bytes 24 | tf_op jit(solution)/shard_map/psum | solution.py:62
  214.8 0.1 multiply_add_fusion.1
  215.0 1.7 collective-permute-start.12
  216.7 0.1 fusion.133
  216.8 1.3 collective-permute-done.13
  218.2 4.0 %collective-permute-start.14 = (f32[3,10,1,128]{3,2,1,0:T(1,128)S(1)}, f32[3,10,1,128]{3,2,1,0:T(1,128)S(1)}, u32[]{:S(2)}, u32[]{:S(2)}) collective-permute-start(f32[3,10,1,128]{3,2,1,0:T(1,128)S(1)} %get-tuple-element.23), channel_id=1, source_target_pairs={{1,0},{2,1},{3,2},{4,3},{5,4},{6,5},{7,6},{0,7},{9,8},{10,9},{11,1... | collective-permute-start | bytes 46088 | tf_op jit(solution)/shard_map/ppermute | solution.py:19
  222.2 0.1 fusion.134
  222.3 1.3 collective-permute-done.14
  223.6 5.0 %collective-permute-done.15 = f32[3,10,1,128]{3,2,1,0:T(1,128)S(1)} collective-permute-done((f32[3,10,1,128]{3,2,1,0:T(1,128)S(1)}, f32[3,10,1,128]{3,2,1,0:T(1,128)S(1)}, u32[]{:S(2)}, u32[]{:S(2)}) %collective-permute-start.15) | collective-permute-done | bytes 15392 | tf_op jit(solution)/shard_map/ppermute | solution.py:16
  228.6 0.2 fusion.7
  228.9 17.1 %psum.70 = f32[3]{0:T(128)S(1)} all-reduce(f32[3]{0:T(128)S(1)} %fusion.7), channel_id=1, replica_groups=mesh['col'=4,'slab'=8] {'slab'}, use_global_device_ids=true, to_apply=%region_13.14 | all-reduce | flops 3 | bytes 24 | tf_op jit(solution)/shard_map/psum | solution.py:99
  246.0 5.7 %psum.71 = f32[3]{0:T(128)S(1)} all-reduce(f32[3]{0:T(128)S(1)} %psum.70), channel_id=1, replica_groups=mesh['col'=4,'slab'=8] {'col'}, use_global_device_ids=true, to_apply=%region_14.15 | all-reduce | flops 3 | bytes 24 | tf_op jit(solution)/shard_map/psum | solution.py:99
  251.7 0.1 multiply_add_fusion
  251.9 0.1 slice.639
  252.0 1.7 collective-permute-start.16
  253.7 0.1 maximum_subtract_fusion.8
  253.8 5.7 %fusion.94 = (f32[8,8,128]{2,1,0:T(8,128)S(1)}, f32[8,8,128]{2,1,0:T(8,128)S(1)}) fusion(f32[8,8,128]{2,1,0:T(8,128)S(1)} %select_multiply_fusion, f32[8,8,1]{2,1,0:T(8,128)S(1)} %bitcast.219, f32[8,8,127]{2,1,0:T(8,128)S(1)} %slice.582, f32[3,8,8,128]{3,2,1,0:T(8,128)S(1)} %maximum_subtract_fusion.8, f32[]{:T(128)} %bitcast.13, f32[]{:T(128)} %bitcast.12, ...), kind=kLoop, calls=%fused_computation.222 | loop fusion | flops 319488 | bytes 327716 | tf_op jit(solution)/shard_map/mul | solution.py:122
  259.5 0.1 slice.644
  259.6 2.1 collective-permute-start.18
  261.8 5.6 %fusion.81 = f32[9,8,128]{2,1,0:T(8,128)S(1)} fusion(f32[3,9,8,128]{3,2,1,0:T(8,128)S(1)} %maximum_subtract_fusion, f32[1,9,8,128]{3,2,1,0:T(8,128)S(1)} %get-tuple-element.16, f32[1,9,8,128]{3,2,1,0:T(8,128)S(1)} %get-tuple-element.15, f32[1,9,8,128]{3,2,1,0:T(8,128)S(1)} %get-tuple-element.14, f32[]{:T(128)} %bitcast.13, f32[]{:T(128)} %bitcast.12, ...), kind=kLoop, calls=%fused_computation.190 | loop fusion | flops 294912 | bytes 258084 | tf_op jit(solution)/shard_map/sub | solution.py:116
  267.4 0.7 collective-permute-done.19
  268.2 5.7 %fusion.62 = f32[8,9,128]{2,1,0:T(8,128)S(1)} fusion(f32[3,8,9,128]{3,2,1,0:T(8,128)S(1)} %fusion, f32[1,8,9,128]{3,2,1,0:T(8,128)S(1)} %fusion.68, f32[1,8,9,128]{3,2,1,0:T(8,128)S(1)} %fusion.69, f32[1,8,9,128]{3,2,1,0:T(8,128)S(1)} %maximum_subtract_fusion.10, f32[]{:T(128)} %bitcast.13, f32[]{:T(128)} %bitcast.12, f32[]{:T(128)} %bitcast.11, ...), kind=kLoop, calls=%fused_computation.137 | loop fusion | flops 294912 | bytes 258084 | tf_op jit(solution)/shard_map/sub | solution.py:116
  273.8 0.7 fusion.101
  (53 shorter events, 1.0 us)
Async XLA Ops:
  0.6 4.0 %copy-start = (f32[3,8,8,128]{3,2,1,0:T(8,128)S(1)}, f32[3,8,8,128]{3,2,1,0:T(8,128)}, u32[]{:S(2)}) copy-start(f32[3,8,8,128]{3,2,1,0:T(8,128)} %param.8) | copy-start | bytes 294916
  4.6 4.4 %collective-permute-start = (f32[4,1,8,128]{3,2,1,0:T(8,128)S(1)}, f32[4,1,8,128]{3,2,1,0:T(8,128)S(1)}, u32[]{:S(2)}, u32[]{:S(2)}) collective-permute-start(f32[4,1,8,128]{3,2,1,0:T(8,128)S(1)} %get-tuple-element.19), channel_id=1, source_target_pairs={{0,8},{8,16},{16,24},{24,0},{1,9},{9,17},{17,25},{25,1},{2,10},{10... | collective-permute-start | bytes 49160 | tf_op jit(solution)/shard_map/ppermute | solution.py:16
  5.1 3.9 %collective-permute-start.1 = (f32[4,1,8,128]{3,2,1,0:T(8,128)S(1)}, f32[4,1,8,128]{3,2,1,0:T(8,128)S(1)}, u32[]{:S(2)}, u32[]{:S(2)}) collective-permute-start(f32[4,1,8,128]{3,2,1,0:T(8,128)S(1)} %get-tuple-element.20), channel_id=1, source_target_pairs={{8,0},{16,8},{24,16},{0,24},{9,1},{17,9},{25,17},{1,25},{10,2},{18... | collective-permute-start | bytes 49160 | tf_op jit(solution)/shard_map/ppermute | solution.py:19
  7.5 0.7 copy-start.2
  9.1 6.8 %collective-permute-start.3 = (f32[4,10,1,128]{3,2,1,0:T(1,128)S(1)}, f32[4,10,1,128]{3,2,1,0:T(1,128)S(1)}, u32[]{:S(2)}, u32[]{:S(2)}) collective-permute-start(f32[4,10,1,128]{3,2,1,0:T(1,128)S(1)} %get-tuple-element.17), channel_id=1, source_target_pairs={{1,0},{2,1},{3,2},{4,3},{5,4},{6,5},{7,6},{0,7},{9,8},{10,9},{11,1... | collective-permute-start | bytes 61448 | tf_op jit(solution)/shard_map/ppermute | solution.py:19
  14.4 6.6 %collective-permute-start.2 = (f32[4,10,1,128]{3,2,1,0:T(1,128)S(1)}, f32[4,10,1,128]{3,2,1,0:T(1,128)S(1)}, u32[]{:S(2)}, u32[]{:S(2)}) collective-permute-start(f32[4,10,1,128]{3,2,1,0:T(1,128)S(1)} %get-tuple-element.18), channel_id=1, source_target_pairs={{0,1},{1,2},{2,3},{3,4},{4,5},{5,6},{6,7},{7,0},{8,9},{9,10},{10,1... | collective-permute-start | bytes 61448 | tf_op jit(solution)/shard_map/ppermute | solution.py:16
  27.1 3.2 %collective-permute-start.5 = (f32[3,1,8,128]{3,2,1,0:T(8,128)S(1)}, f32[3,1,8,128]{3,2,1,0:T(8,128)S(1)}, u32[]{:S(2)}, u32[]{:S(2)}) collective-permute-start(f32[3,1,8,128]{3,2,1,0:T(8,128)S(1)} %get-tuple-element.43), channel_id=1, source_target_pairs={{0,8},{8,16},{16,24},{24,0},{1,9},{9,17},{17,25},{25,1},{2,10},{10... | collective-permute-start | bytes 36872 | tf_op jit(solution)/shard_map/ppermute | solution.py:16
  27.2 3.1 %collective-permute-start.4 = (f32[3,1,8,128]{3,2,1,0:T(8,128)S(1)}, f32[3,1,8,128]{3,2,1,0:T(8,128)S(1)}, u32[]{:S(2)}, u32[]{:S(2)}) collective-permute-start(f32[3,1,8,128]{3,2,1,0:T(8,128)S(1)} %get-tuple-element.44), channel_id=1, source_target_pairs={{8,0},{16,8},{24,16},{0,24},{9,1},{17,9},{25,17},{1,25},{10,2},{18... | collective-permute-start | bytes 36872 | tf_op jit(solution)/shard_map/ppermute | solution.py:19
  30.4 3.8 %collective-permute-start.6 = (f32[3,10,1,128]{3,2,1,0:T(1,128)S(1)}, f32[3,10,1,128]{3,2,1,0:T(1,128)S(1)}, u32[]{:S(2)}, u32[]{:S(2)}) collective-permute-start(f32[3,10,1,128]{3,2,1,0:T(1,128)S(1)} %get-tuple-element.27), channel_id=1, source_target_pairs={{1,0},{2,1},{3,2},{4,3},{5,4},{6,5},{7,6},{0,7},{9,8},{10,9},{11,1... | collective-permute-start | bytes 46088 | tf_op jit(solution)/shard_map/ppermute | solution.py:19
  30.4 6.5 %collective-permute-start.7 = (f32[3,10,1,128]{3,2,1,0:T(1,128)S(1)}, f32[3,10,1,128]{3,2,1,0:T(1,128)S(1)}, u32[]{:S(2)}, u32[]{:S(2)}) collective-permute-start(f32[3,10,1,128]{3,2,1,0:T(1,128)S(1)} %get-tuple-element.28), channel_id=1, source_target_pairs={{0,1},{1,2},{2,3},{3,4},{4,5},{5,6},{6,7},{7,0},{8,9},{9,10},{10,1... | collective-permute-start | bytes 46088 | tf_op jit(solution)/shard_map/ppermute | solution.py:16
  139.9 3.2 %collective-permute-start.9 = (f32[3,1,8,128]{3,2,1,0:T(8,128)S(1)}, f32[3,1,8,128]{3,2,1,0:T(8,128)S(1)}, u32[]{:S(2)}, u32[]{:S(2)}) collective-permute-start(f32[3,1,8,128]{3,2,1,0:T(8,128)S(1)} %get-tuple-element.37), channel_id=1, source_target_pairs={{0,8},{8,16},{16,24},{24,0},{1,9},{9,17},{17,25},{25,1},{2,10},{10... | collective-permute-start | bytes 36872 | tf_op jit(solution)/shard_map/ppermute | solution.py:16
  140.0 3.1 %collective-permute-start.8 = (f32[3,1,8,128]{3,2,1,0:T(8,128)S(1)}, f32[3,1,8,128]{3,2,1,0:T(8,128)S(1)}, u32[]{:S(2)}, u32[]{:S(2)}) collective-permute-start(f32[3,1,8,128]{3,2,1,0:T(8,128)S(1)} %get-tuple-element.38), channel_id=1, source_target_pairs={{8,0},{16,8},{24,16},{0,24},{9,1},{17,9},{25,17},{1,25},{10,2},{18... | collective-permute-start | bytes 36872 | tf_op jit(solution)/shard_map/ppermute | solution.py:19
  143.2 4.8 %collective-permute-start.10 = (f32[3,10,1,128]{3,2,1,0:T(1,128)S(1)}, f32[3,10,1,128]{3,2,1,0:T(1,128)S(1)}, u32[]{:S(2)}, u32[]{:S(2)}) collective-permute-start(f32[3,10,1,128]{3,2,1,0:T(1,128)S(1)} %get-tuple-element.25), channel_id=1, source_target_pairs={{1,0},{2,1},{3,2},{4,3},{5,4},{6,5},{7,6},{0,7},{9,8},{10,9},{11,1... | collective-permute-start | bytes 46088 | tf_op jit(solution)/shard_map/ppermute | solution.py:19
  146.5 6.4 %collective-permute-start.11 = (f32[3,10,1,128]{3,2,1,0:T(1,128)S(1)}, f32[3,10,1,128]{3,2,1,0:T(1,128)S(1)}, u32[]{:S(2)}, u32[]{:S(2)}) collective-permute-start(f32[3,10,1,128]{3,2,1,0:T(1,128)S(1)} %get-tuple-element.26), channel_id=1, source_target_pairs={{0,1},{1,2},{2,3},{3,4},{4,5},{5,6},{6,7},{7,0},{8,9},{9,10},{10,1... | collective-permute-start | bytes 46088 | tf_op jit(solution)/shard_map/ppermute | solution.py:16
  214.9 3.2 %collective-permute-start.13 = (f32[3,1,8,128]{3,2,1,0:T(8,128)S(1)}, f32[3,1,8,128]{3,2,1,0:T(8,128)S(1)}, u32[]{:S(2)}, u32[]{:S(2)}) collective-permute-start(f32[3,1,8,128]{3,2,1,0:T(8,128)S(1)} %get-tuple-element.35), channel_id=1, source_target_pairs={{0,8},{8,16},{16,24},{24,0},{1,9},{9,17},{17,25},{25,1},{2,10},{10... | collective-permute-start | bytes 36872 | tf_op jit(solution)/shard_map/ppermute | solution.py:16
  215.0 3.1 %collective-permute-start.12 = (f32[3,1,8,128]{3,2,1,0:T(8,128)S(1)}, f32[3,1,8,128]{3,2,1,0:T(8,128)S(1)}, u32[]{:S(2)}, u32[]{:S(2)}) collective-permute-start(f32[3,1,8,128]{3,2,1,0:T(8,128)S(1)} %get-tuple-element.36), channel_id=1, source_target_pairs={{8,0},{16,8},{24,16},{0,24},{9,1},{17,9},{25,17},{1,25},{10,2},{18... | collective-permute-start | bytes 36872 | tf_op jit(solution)/shard_map/ppermute | solution.py:19
  218.2 5.5 %collective-permute-start.14 = (f32[3,10,1,128]{3,2,1,0:T(1,128)S(1)}, f32[3,10,1,128]{3,2,1,0:T(1,128)S(1)}, u32[]{:S(2)}, u32[]{:S(2)}) collective-permute-start(f32[3,10,1,128]{3,2,1,0:T(1,128)S(1)} %get-tuple-element.23), channel_id=1, source_target_pairs={{1,0},{2,1},{3,2},{4,3},{5,4},{6,5},{7,6},{0,7},{9,8},{10,9},{11,1... | collective-permute-start | bytes 46088 | tf_op jit(solution)/shard_map/ppermute | solution.py:19
  222.2 6.4 %collective-permute-start.15 = (f32[3,10,1,128]{3,2,1,0:T(1,128)S(1)}, f32[3,10,1,128]{3,2,1,0:T(1,128)S(1)}, u32[]{:S(2)}, u32[]{:S(2)}) collective-permute-start(f32[3,10,1,128]{3,2,1,0:T(1,128)S(1)} %get-tuple-element.24), channel_id=1, source_target_pairs={{0,1},{1,2},{2,3},{3,4},{4,5},{5,6},{6,7},{7,0},{8,9},{9,10},{10,1... | collective-permute-start | bytes 46088 | tf_op jit(solution)/shard_map/ppermute | solution.py:16
  251.8 16.3 %copy-start.1 = (f32[3,8,8,128]{3,2,1,0:T(8,128)}, f32[3,8,8,128]{3,2,1,0:T(8,128)S(1)}, u32[]{:S(2)}) copy-start(f32[3,8,8,128]{3,2,1,0:T(8,128)S(1)} %multiply_add_fusion) | copy-start | bytes 294916
  251.9 7.7 %collective-permute-start.17 = (f32[3,1,8,128]{3,2,1,0:T(8,128)S(1)}, f32[3,1,8,128]{3,2,1,0:T(8,128)S(1)}, u32[]{:S(2)}, u32[]{:S(2)}) collective-permute-start(f32[3,1,8,128]{3,2,1,0:T(8,128)S(1)} %get-tuple-element.29), channel_id=1, source_target_pairs={{0,8},{8,16},{16,24},{24,0},{1,9},{9,17},{17,25},{25,1},{2,10},{10... | collective-permute-start | bytes 36872 | tf_op jit(solution)/shard_map/ppermute | solution.py:16
  252.0 7.6 %collective-permute-start.16 = (f32[3,1,8,128]{3,2,1,0:T(8,128)S(1)}, f32[3,1,8,128]{3,2,1,0:T(8,128)S(1)}, u32[]{:S(2)}, u32[]{:S(2)}) collective-permute-start(f32[3,1,8,128]{3,2,1,0:T(8,128)S(1)} %get-tuple-element.30), channel_id=1, source_target_pairs={{8,0},{16,8},{24,16},{0,24},{9,1},{17,9},{25,17},{1,25},{10,2},{18... | collective-permute-start | bytes 36872 | tf_op jit(solution)/shard_map/ppermute | solution.py:19
  259.6 7.8 %collective-permute-start.18 = (f32[3,10,1,128]{3,2,1,0:T(1,128)S(1)}, f32[3,10,1,128]{3,2,1,0:T(1,128)S(1)}, u32[]{:S(2)}, u32[]{:S(2)}) collective-permute-start(f32[3,10,1,128]{3,2,1,0:T(1,128)S(1)} %get-tuple-element.21), channel_id=1, source_target_pairs={{1,0},{2,1},{3,2},{4,3},{5,4},{6,5},{7,6},{0,7},{9,8},{10,9},{11,1... | collective-permute-start | bytes 46088 | tf_op jit(solution)/shard_map/ppermute | solution.py:19
  261.7 6.4 %collective-permute-start.19 = (f32[3,10,1,128]{3,2,1,0:T(1,128)S(1)}, f32[3,10,1,128]{3,2,1,0:T(1,128)S(1)}, u32[]{:S(2)}, u32[]{:S(2)}) collective-permute-start(f32[3,10,1,128]{3,2,1,0:T(1,128)S(1)} %get-tuple-element.22), channel_id=1, source_target_pairs={{0,1},{1,2},{2,3},{3,4},{4,5},{5,6},{6,7},{7,0},{8,9},{9,10},{10,1... | collective-permute-start | bytes 46088 | tf_op jit(solution)/shard_map/ppermute | solution.py:16
